TPU v7x, 512 devices: a whole 4x8x8 slice. The times are simulated.
512 devices in a mesh: row: 32 (over y, x), col: 16 (over z, core).
Axes of the slice: x: 4, y: 8, z: 8, core: 2. Of those that a mesh axis runs over, the one named last changes fastest.
Arguments:
- kernel_matrix: float32 [16384, 16384], P('row', 'col'), may hold values from 0 to 2, as said below
Outputs:
- factored: float32 [16384, 16384], P('row', 'col')
Inputs may be any that keep to these rules, and one draw needn't show every extreme that they name: kernel_matrix, put in global order by the element-cyclic map, is symmetric: a Gaussian-process kernel amp * exp(-distance / scale) over random points plus a nugget of at least 0.5 on the diagonal, so it is positive definite with smallest eigenvalue at least 0.5.
All inputs are finite; a program needn't handle non-finite values.
Results may differ from a plain program's by a relative error of at most 0.00025.
Values sent between devices are 32-bit elements; how exact they have to be, the bound alone decides.
No kernel may reach another device: no remote copies, remote signals or barrier semaphores. Data moves between devices by JAX's collectives and lax.ppermute only.
A program may use at most 64 MiB of HBM per device.

v0:
```python
import jax
import jax.numpy as jnp
from jax import lax
from jax.sharding import PartitionSpec as P

PANEL = 192
PANELS = 2


def spread(block, axis, source):
    block = jnp.where(lax.axis_index(axis) == source, block, jnp.zeros_like(block))
    return lax.psum(block, axis)


def solve_rows(lower_factor, rows):
    return lax.linalg.triangular_solve(
        lower_factor, rows, left_side=False, lower=True, transpose_a=True
    )


def alternate_cols(block, groups):
    height = block.shape[0]
    inner = block.shape[1] // groups
    return block.reshape(height, groups, inner).transpose(0, 2, 1).reshape(height, groups * inner)


def alternate_rows(block, groups):
    inner = block.shape[0] // groups
    breadth = block.shape[1]
    return block.reshape(groups, inner, breadth).transpose(1, 0, 2).reshape(groups * inner, breadth)


def per_device(kernel_matrix):
    matrix = kernel_matrix
    row_count = lax.axis_size("row")
    col_count = lax.axis_size("col")
    row_share = row_count // col_count
    local_rows, local_cols = matrix.shape
    tile_rows = PANEL // row_count
    tile_cols = PANEL // col_count
    col_index = lax.axis_index("col")
    for current in range(PANELS):
        factor_row_start = current * tile_rows
        factor_col_start = current * tile_cols
        factor_col_rest = factor_col_start + tile_cols
        corner = matrix[
            factor_row_start : factor_row_start + tile_rows, factor_col_start:factor_col_rest
        ]
        corner = lax.all_gather(corner, "row", axis=0, tiled=True)
        corner = lax.all_gather(corner, "col", axis=1, tiled=True)
        corner = alternate_cols(alternate_rows(corner, row_count), col_count)
        lower_factor = jnp.linalg.cholesky(corner)
        column_block = matrix[:, factor_col_start:factor_col_rest]
        gathered = alternate_cols(
            lax.all_gather(column_block, "col", axis=1, tiled=True), col_count
        )
        factor_left_rows = solve_rows(lower_factor, gathered)
        received = []
        for source in range(row_share):
            received.append(spread(factor_left_rows, "row", col_index + source * col_count))
        factor_right_rows = jnp.stack(received, axis=1).reshape(local_cols, PANEL)[factor_col_rest:]
        row_start = current * tile_rows
        col_start = current * tile_cols
        owned = factor_left_rows.reshape(local_rows, tile_cols, col_count)
        owned = lax.dynamic_index_in_dim(owned, col_index, axis=2, keepdims=False)
        matrix = matrix.at[row_start:, col_start : col_start + tile_cols].set(owned[row_start:])
        row_low = (current + 1) * tile_rows
        col_low = (current + 1) * tile_cols
        term = jnp.dot(
            factor_left_rows[row_low:local_rows],
            factor_right_rows.T,
            precision=lax.Precision.HIGHEST,
            preferred_element_type=jnp.float32,
        )
        matrix = matrix.at[row_low:local_rows, col_low:local_cols].add(-term)
    return matrix


def solution(mesh):
    in_specs = (P("row", "col"),)
    out_specs = P("row", "col")
    return jax.shard_map(
        per_device, mesh=mesh, in_specs=in_specs, out_specs=out_specs, check_vma=False
    )
```

profile of v0, /device:TPU:16, one launch (start us, length us, event | category | flops | bytes accessed | tf_op | source)
XLA Modules:
  0.0 630.4 jit_solution(13229825803608452660)
XLA Ops:
  6.5 1.9 copy.35
  8.5 0.7 slice_bitcast_fusion.12
  9.2 24.6 %all-gather.2 = f32[16,12,512]{2,1,0:T(8,128)S(1)} all-gather(f32[1,12,512]{2,1,0:T(8,128)S(1)} %slice_bitcast_fusion.11), channel_id=1, replica_groups=mesh['row'=32,'col'=16] {'col'}, dimensions={0}, use_global_device_ids=true | all-gather | bytes 417792 | tf_op jit(solution)/shard_map/all_gather | solution.py:55
  34.1 39.3 %all-gather = f32[32,6,12]{2,1,0:T(8,128)S(1)} all-gather(f32[1,6,12]{2,1,0:T(8,128)S(1)} %slice_bitcast_fusion.12), channel_id=1, replica_groups=mesh['row'=32,'col'=16] {'row'}, dimensions={0}, use_global_device_ids=true | all-gather | bytes 9504 | tf_op jit(solution)/shard_map/all_gather | solution.py:49
  73.5 14.9 %all-gather.1 = f32[16,12,192]{2,1,0:T(8,128)S(1)} all-gather(f32[1,12,192]{2,1,0:T(8,128)S(1)} %bitcast.133), channel_id=1, replica_groups=mesh['row'=32,'col'=16] {'col'}, dimensions={0}, use_global_device_ids=true | all-gather | bytes 156672 | tf_op jit(solution)/shard_map/all_gather | solution.py:50
  88.5 0.3 copy.30
  89.4 11.7 %cholesky.136 = f32[128,128]{1,0:T(8,128)S(1)} custom-call(f32[128,128]{1,0:T(8,128)S(1)} %cholesky.208), custom_call_target="Cholesky" | custom-call | tf_op jit(solution)/shard_map/jit(cholesky)/cholesky | solution.py:52
  101.1 9.8 %custom-call.13 = f32[1,128,128]{1,2,0:T(8,128)S(1)} custom-call(f32[1,128,128]{2,1,0:T(8,128)S(1)} %get-tuple-element.94), custom_call_target="InvertDiagBlocksLowerTriangular" | custom-call | tf_op jit(solution)/shard_map/jit(cholesky)/cholesky | solution.py:52
  111.3 5.8 cholesky.156
  117.2 0.6 compare_reduce_fusion.3
  117.8 0.7 compare_reduce_fusion.2
  120.0 0.6 copy-done.1
  120.7 19.7 %custom-call.14 = f32[2,128,128]{1,2,0:T(8,128)S(1)} custom-call(f32[2,128,128]{2,1,0:T(8,128)S(1)} %pad_maximum_fusion.4), custom_call_target="InvertDiagBlocksLowerTriangular" | custom-call | tf_op jit(solution)/shard_map/triangular_solve/custom-call.0 | solution.py:16
  140.4 0.6 copy-done.3
  141.0 0.4 fusion.6
  141.8 1.1 fusion.19
  142.9 1.0 select_bitcast_fusion.3
  144.1 0.6 compare_reduce_fusion.4
  144.8 0.6 bitcast_select_fusion
  145.4 0.3 scatter.6
  145.7 153.4 %all-reduce.10.cloned.1.call-done = (f32[512,1,192]{0,2,1:T(8,128)}, f32[512,1,192]{0,2,1:T(8,128)}) async-done(((f32[512,1,192]{0,2,1:T(8,128)}, f32[512,1,192]{0,2,1:T(8,128)}), (f32[512,1,192]{0,2,1:T(8,128)}, f32[512,1,192]{0,2,1:T(8,128)})) %all-reduce.10.cloned.1.call-update) | async-done | bytes 786448 | tf_op jit(solution)/shard_map/psum | solution.py:12
  299.1 1.4 pad_maximum_fusion.1
  300.5 1.3 copy.36
  301.8 1.9 slice.169
  303.8 2.1 slice_add_fusion
  305.8 1.3 copy-done
  307.2 36.3 %all-gather.3 = f32[32,6,12]{2,1,0:T(8,128)S(1)} all-gather(f32[1,6,12]{2,1,0:T(8,128)S(1)} %bitcast.135), channel_id=1, replica_groups=mesh['row'=32,'col'=16] {'row'}, dimensions={0}, use_global_device_ids=true | all-gather | bytes 9504 | tf_op jit(solution)/shard_map/all_gather | solution.py:49
  343.6 18.8 %all-gather.4 = f32[16,12,192]{2,1,0:T(8,128)S(1)} all-gather(f32[1,12,192]{2,1,0:T(8,128)S(1)} %bitcast.134), channel_id=1, replica_groups=mesh['row'=32,'col'=16] {'col'}, dimensions={0}, use_global_device_ids=true | all-gather | bytes 156672 | tf_op jit(solution)/shard_map/all_gather | solution.py:50
  362.6 0.3 copy.40
  363.4 11.7 %cholesky.174 = f32[128,128]{1,0:T(8,128)S(1)} custom-call(f32[128,128]{1,0:T(8,128)S(1)} %cholesky.211), custom_call_target="Cholesky" | custom-call | tf_op jit(solution)/shard_map/jit(cholesky)/cholesky | solution.py:52
  375.2 9.8 %custom-call.15 = f32[1,128,128]{1,2,0:T(8,128)S(1)} custom-call(f32[1,128,128]{2,1,0:T(8,128)S(1)} %get-tuple-element.92), custom_call_target="InvertDiagBlocksLowerTriangular" | custom-call | tf_op jit(solution)/shard_map/jit(cholesky)/cholesky | solution.py:52
  385.4 5.8 cholesky.194
  391.3 0.7 compare_reduce_fusion.1
  392.0 0.6 compare_reduce_fusion
  394.0 10.9 %scatter-add.6 = f32[512,1024]{0,1:T(8,128)S(1)} dynamic-update-slice(f32[512,1024]{0,1:T(8,128)S(1)} %scatter.6, f32[506,1012]{0,1:T(8,128)} %copy-done, s32[]{:T(128)} %constant.182.clone.1, s32[]{:T(128)} %constant.183.clone.1) | dynamic-update-slice | bytes 4096580 | tf_op jit(solution)/shard_map/scatter-add | solution.py:75
  404.9 16.4 %all-gather.5 = f32[16,12,512]{2,1,0:T(8,128)S(1)} all-gather(f32[1,12,512]{2,1,0:T(8,128)S(1)} %slice_bitcast_fusion.8), channel_id=1, replica_groups=mesh['row'=32,'col'=16] {'col'}, dimensions={0}, use_global_device_ids=true | all-gather | bytes 417792 | tf_op jit(solution)/shard_map/all_gather | solution.py:55
  421.7 19.7 %custom-call.16 = f32[2,128,128]{1,2,0:T(8,128)S(1)} custom-call(f32[2,128,128]{2,1,0:T(8,128)S(1)} %pad_maximum_fusion.5), custom_call_target="InvertDiagBlocksLowerTriangular" | custom-call | tf_op jit(solution)/shard_map/triangular_solve/custom-call.0 | solution.py:16
  441.4 0.4 fusion.4
  442.1 0.3 fusion.16
  442.4 1.0 select_bitcast_fusion.1
  443.6 1.1 scatter.9
  444.7 155.9 %all-reduce.8.cloned.1.call-done = (f32[512,1,192]{0,2,1:T(8,128)}, f32[512,1,192]{0,2,1:T(8,128)}) async-done(((f32[512,1,192]{0,2,1:T(8,128)}, f32[512,1,192]{0,2,1:T(8,128)}), (f32[512,1,192]{0,2,1:T(8,128)}, f32[512,1,192]{0,2,1:T(8,128)})) %all-reduce.8.cloned.1.call-update) | async-done | bytes 786448 | tf_op jit(solution)/shard_map/psum | solution.py:12
  600.6 2.3 pad_maximum_fusion
  602.9 1.9 copy.45
  604.8 1.7 slice.176
  606.5 4.5 slice_add_fusion.1
  611.0 10.8 %scatter-add.9 = f32[512,1024]{0,1:T(8,128)S(1)} dynamic-update-slice(f32[512,1024]{0,1:T(8,128)S(1)} %scatter.9, f32[500,1000]{0,1:T(8,128)} %slice_add_fusion.1, s32[]{:T(128)} %constant.183.clone.1, s32[]{:T(128)} %constant.184.clone.1) | dynamic-update-slice | bytes 4000004 | tf_op jit(solution)/shard_map/scatter-add | solution.py:75
  621.8 1.8 copy.46
  (65 shorter events, 4.4 us)
Async XLA Ops:
  6.5 292.6 %all-reduce.10.cloned.1.call-start = ((), (), s32[]{:S(2)}) async-start(), calls=%async_computation.1 | async-start | bytes 1572864 | tf_op jit(solution)/shard_map/psum | solution.py:12
  120.0 0.6 copy-start.1
  140.4 0.7 copy-start.3
  143.9 456.7 %all-reduce.8.cloned.1.call-start = ((), (), s32[]{:S(2)}) async-start(), calls=%async_computation | async-start | bytes 1572864 | tf_op jit(solution)/shard_map/psum | solution.py:12
  305.8 1.3 copy-start
  404.8 16.7 %copy-start.2 = (f32[128,64]{1,0:T(8,128)S(1)}, f32[128,64]{1,0:T(8,128)}, u32[]{:S(2)}) copy-start(f32[128,64]{1,0:T(8,128)} %copy-done.1) | copy-start | bytes 98308
Sparse Core Ops, SparseCore 0:
  144.0 155.0 all-reduce.9
  443.6 156.9 all-reduce.7
where the time goes:
time: 631 us; the launch traced here: 630 us
  waiting for transfers between devices  309 us (49%)
  blocking collectives  150 us (24%)
  other arithmetic  104 us (16%)
  local copies, waits for them, and re-layouts  39.9 us (6%)
  between operations  16.5 us (3%)
  matrix products  10.2 us (2%)
    psum x2, waiting for transfers between devices, spread(): return lax.psum(block, axis)  309 us
    all_gather x2, blocking collectives, per_device(): corner = lax.all_gather(corner, 'row', axis=0, tiled=True)  75.6 us
    another operation x14, other arithmetic, per_device(): lower_factor = jnp.linalg.cholesky(corner)  57.6 us
    all_gather x2, blocking collectives, per_device(): lax.all_gather(column_block, 'col', axis=1, tiled=True)  41 us
    another operation x10, other arithmetic, solve_rows(): lax.linalg.triangular_solve(lower_factor, rows, left_side=False, lower=Tr...  39.6 us
    all_gather x2, blocking collectives, per_device(): corner = lax.all_gather(corner, 'col', axis=1, tiled=True)  33.6 us
    scatter-add x3, local copies, waits for them, and re-layouts, per_device(): matrix = matrix.at[row_low:local_rows, col_low:local_cols].add(-term)  23.4 us
  transfers between devices with their start and end apart: 2, of which 2 were waited for; matrix products, arithmetic and copies ran while one was open for 0% of the time, Pallas kernels for 0%

commit v1 on v0

--- a/solution.py
+++ b/solution.py
@@ -5,6 +5,13 @@
 
 PANEL = 192
 PANELS = 2
+
+
+def exchange_gather(block, axis, d):
+    count = lax.axis_size(axis)
+    blocks = jnp.stack([block for _ in range(count)])
+    blocks = lax.all_to_all(blocks, axis, split_axis=0, concat_axis=0)
+    return jnp.concatenate(blocks, axis=d)
 
 
 def spread(block, axis, source):
@@ -46,7 +53,7 @@
         corner = matrix[
             factor_row_start : factor_row_start + tile_rows, factor_col_start:factor_col_rest
         ]
-        corner = lax.all_gather(corner, "row", axis=0, tiled=True)
+        corner = exchange_gather(corner, "row", 0)
         corner = lax.all_gather(corner, "col", axis=1, tiled=True)
         corner = alternate_cols(alternate_rows(corner, row_count), col_count)
         lower_factor = jnp.linalg.cholesky(corner)

time: 631 us -> 577 us (0.914)
  blocking collectives: 150 us -> 74.9 us
  starting transfers between devices: 0.22 us -> 16.8 us
    all_gather x2 -> x0, blocking collectives: 75.6 us -> none  [per_device(): corner = lax.all_gather(corner, 'row', axis=0, tiled=True)]
    all_to_all x0 -> x2, starting transfers between devices: none -> 16.7 us  [exchange_gather(): blocks = lax.all_to_all(blocks, axis, split_axis=0, concat_axis=0)]
  transfers between devices with their start and end apart: 2 -> 4, of which waited for: 2 -> 2; matrix products, arithmetic and copies ran while one was open for 0% -> 1% of each run, Pallas kernels for 0% -> 0%
where the time goes in v1:
time: 577 us; the launch traced here: 576 us
  waiting for transfers between devices  314 us (54%)
  other arithmetic  105 us (18%)
  blocking collectives  74.9 us (13%)
  local copies, waits for them, and re-layouts  39.9 us (7%)
  starting transfers between devices  16.8 us (3%)
  between operations  16.7 us (3%)
  matrix products  9.39 us (2%)
    psum x2, waiting for transfers between devices, spread(): return lax.psum(block, axis)  314 us
    another operation x14, other arithmetic, per_device(): lower_factor = jnp.linalg.cholesky(corner)  57.6 us
    all_gather x2, blocking collectives, per_device(): lax.all_gather(column_block, 'col', axis=1, tiled=True)  44.1 us
    another operation x10, other arithmetic, solve_rows(): lax.linalg.triangular_solve(lower_factor, rows, left_side=False, lower=Tr...  40.7 us
    all_gather x2, blocking collectives, per_device(): corner = lax.all_gather(corner, 'col', axis=1, tiled=True)  30.8 us
    scatter-add x3, local copies, waits for them, and re-layouts, per_device(): matrix = matrix.at[row_low:local_rows, col_low:local_cols].add(-term)  23.4 us
    all_to_all x2, starting transfers between devices, exchange_gather(): blocks = lax.all_to_all(blocks, axis, split_axis=0, concat_axis=0)  16.7 us
  transfers between devices with their start and end apart: 4, of which 2 were waited for; matrix products, arithmetic and copies ran while one was open for 1% of the time, Pallas kernels for 0%

profile of v1, /device:TPU:16, one launch (start us, length us, event | category | flops | bytes accessed | tf_op | source)
XLA Modules:
  0.0 576.4 jit_solution(11028482352208780487)
XLA Ops:
  6.5 0.7 slice.164
  7.2 0.7 stack.16
  7.9 10.1 %all-to-all-start = ((f32[32,6,12]{2,1,0:T(8,128)}), f32[32,6,12]{2,1,0:T(8,128)S(1)}, u32[]{:S(2)}, u32[]{:S(2)}) async-start(f32[32,6,12]{2,1,0:T(8,128)} %stack.16), calls=%async_computation | async-start | bytes 262144 | tf_op jit(solution)/shard_map/all_to_all | solution.py:13
  18.0 1.9 copy.33
  20.0 24.6 %all-gather.1 = f32[16,12,512]{2,1,0:T(8,128)S(1)} all-gather(f32[1,12,512]{2,1,0:T(8,128)S(1)} %slice_bitcast_fusion.11), channel_id=1, replica_groups=mesh['row'=32,'col'=16] {'col'}, dimensions={0}, use_global_device_ids=true | all-gather | bytes 417792 | tf_op jit(solution)/shard_map/all_gather | solution.py:62
  44.6 0.6 pad_convert_fusion
  45.6 15.2 %all-gather = f32[16,12,192]{2,1,0:T(8,128)S(1)} all-gather(f32[1,12,192]{2,1,0:T(8,128)S(1)} %bitcast.130), channel_id=1, replica_groups=mesh['row'=32,'col'=16] {'col'}, dimensions={0}, use_global_device_ids=true | all-gather | bytes 156672 | tf_op jit(solution)/shard_map/all_gather | solution.py:57
  61.0 0.3 copy.28
  61.9 11.7 %cholesky.136 = f32[128,128]{1,0:T(8,128)S(1)} custom-call(f32[128,128]{1,0:T(8,128)S(1)} %cholesky.208), custom_call_target="Cholesky" | custom-call | tf_op jit(solution)/shard_map/jit(cholesky)/cholesky | solution.py:59
  73.6 9.8 %custom-call.13 = f32[1,128,128]{1,2,0:T(8,128)S(1)} custom-call(f32[1,128,128]{2,1,0:T(8,128)S(1)} %get-tuple-element.94), custom_call_target="InvertDiagBlocksLowerTriangular" | custom-call | tf_op jit(solution)/shard_map/jit(cholesky)/cholesky | solution.py:59
  83.8 5.8 %cholesky.156 = f32[64,64]{1,0:T(8,128)S(1)} custom-call(f32[64,64]{1,0:T(8,128)S(1)} %convolution_subtract_fusion.3), custom_call_target="Cholesky" | custom-call | tf_op jit(solution)/shard_map/jit(cholesky)/cholesky | solution.py:59
  89.7 0.6 compare_reduce_fusion.3
  90.3 0.7 compare_reduce_fusion.2
  92.6 19.9 %custom-call.14 = f32[2,128,128]{1,2,0:T(8,128)S(1)} custom-call(f32[2,128,128]{2,1,0:T(8,128)S(1)} %pad_maximum_fusion.4), custom_call_target="InvertDiagBlocksLowerTriangular" | custom-call | tf_op jit(solution)/shard_map/triangular_solve/custom-call.0 | solution.py:23
  112.4 0.4 fusion.6
  113.2 0.3 fusion.19
  113.5 1.0 select_bitcast_fusion.3
  114.5 0.6 compare_reduce_fusion.4
  115.2 0.6 bitcast_select_fusion
  115.8 0.3 scatter.6
  116.1 155.6 %all-reduce.10.cloned.1.call-done = (f32[512,1,192]{0,2,1:T(8,128)}, f32[512,1,192]{0,2,1:T(8,128)}) async-done(((f32[512,1,192]{0,2,1:T(8,128)}, f32[512,1,192]{0,2,1:T(8,128)}), (f32[512,1,192]{0,2,1:T(8,128)}, f32[512,1,192]{0,2,1:T(8,128)})) %all-reduce.10.cloned.1.call-update) | async-done | bytes 786448 | tf_op jit(solution)/shard_map/psum | solution.py:19
  271.8 1.4 pad_maximum_fusion.1
  273.1 1.3 copy.34
  274.5 1.9 slice.169
  276.4 2.1 slice_add_fusion
  278.5 1.3 copy-done
  279.8 10.8 %scatter-add.6 = f32[512,1024]{0,1:T(8,128)S(1)} dynamic-update-slice(f32[512,1024]{0,1:T(8,128)S(1)} %scatter.6, f32[506,1012]{0,1:T(8,128)} %copy-done, s32[]{:T(128)} %constant.182.clone.1, s32[]{:T(128)} %constant.183.clone.1) | dynamic-update-slice | bytes 4096580 | tf_op jit(solution)/shard_map/scatter-add | solution.py:82
  290.7 0.7 stack.20
  291.4 6.7 %all-to-all-start.1 = ((f32[32,6,12]{2,1,0:T(8,128)}), f32[32,6,12]{2,1,0:T(8,128)S(1)}, u32[]{:S(2)}, u32[]{:S(2)}) async-start(f32[32,6,12]{2,1,0:T(8,128)} %stack.20), calls=%async_computation.1 | async-start | bytes 262144 | tf_op jit(solution)/shard_map/all_to_all | solution.py:13
  298.1 19.5 %all-gather.3 = f32[16,12,512]{2,1,0:T(8,128)S(1)} all-gather(f32[1,12,512]{2,1,0:T(8,128)S(1)} %slice_bitcast_fusion.8), channel_id=1, replica_groups=mesh['row'=32,'col'=16] {'col'}, dimensions={0}, use_global_device_ids=true | all-gather | bytes 417792 | tf_op jit(solution)/shard_map/all_gather | solution.py:62
  318.1 15.6 %all-gather.2 = f32[16,12,192]{2,1,0:T(8,128)S(1)} all-gather(f32[1,12,192]{2,1,0:T(8,128)S(1)} %bitcast.131), channel_id=1, replica_groups=mesh['row'=32,'col'=16] {'col'}, dimensions={0}, use_global_device_ids=true | all-gather | bytes 156672 | tf_op jit(solution)/shard_map/all_gather | solution.py:57
  333.9 0.3 copy.38
  334.8 11.7 %cholesky.174 = f32[128,128]{1,0:T(8,128)S(1)} custom-call(f32[128,128]{1,0:T(8,128)S(1)} %cholesky.211), custom_call_target="Cholesky" | custom-call | tf_op jit(solution)/shard_map/jit(cholesky)/cholesky | solution.py:59
  346.5 9.8 %custom-call.15 = f32[1,128,128]{1,2,0:T(8,128)S(1)} custom-call(f32[1,128,128]{2,1,0:T(8,128)S(1)} %get-tuple-element.92), custom_call_target="InvertDiagBlocksLowerTriangular" | custom-call | tf_op jit(solution)/shard_map/jit(cholesky)/cholesky | solution.py:59
  356.7 5.8 %cholesky.194 = f32[64,64]{1,0:T(8,128)S(1)} custom-call(f32[64,64]{1,0:T(8,128)S(1)} %convolution_subtract_fusion.2), custom_call_target="Cholesky" | custom-call | tf_op jit(solution)/shard_map/jit(cholesky)/cholesky | solution.py:59
  362.6 0.6 compare_reduce_fusion.1
  363.3 0.7 compare_reduce_fusion
  365.5 19.9 %custom-call.16 = f32[2,128,128]{1,2,0:T(8,128)S(1)} custom-call(f32[2,128,128]{2,1,0:T(8,128)S(1)} %pad_maximum_fusion.5), custom_call_target="InvertDiagBlocksLowerTriangular" | custom-call | tf_op jit(solution)/shard_map/triangular_solve/custom-call.0 | solution.py:23
  385.4 0.4 fusion.4
  386.5 1.0 select_bitcast_fusion.1
  387.7 1.1 scatter.9
  388.8 157.9 %all-reduce.8.cloned.1.call-done = (f32[512,1,192]{0,2,1:T(8,128)}, f32[512,1,192]{0,2,1:T(8,128)}) async-done(((f32[512,1,192]{0,2,1:T(8,128)}, f32[512,1,192]{0,2,1:T(8,128)}), (f32[512,1,192]{0,2,1:T(8,128)}, f32[512,1,192]{0,2,1:T(8,128)})) %all-reduce.8.cloned.1.call-update) | async-done | bytes 786448 | tf_op jit(solution)/shard_map/psum | solution.py:19
  546.7 2.3 pad_maximum_fusion
  548.9 1.9 copy.43
  550.8 1.7 slice.176
  552.5 4.5 slice_add_fusion.1
  557.0 10.8 %scatter-add.9 = f32[512,1024]{0,1:T(8,128)S(1)} dynamic-update-slice(f32[512,1024]{0,1:T(8,128)S(1)} %scatter.9, f32[500,1000]{0,1:T(8,128)} %slice_add_fusion.1, s32[]{:T(128)} %constant.183.clone.1, s32[]{:T(128)} %constant.184.clone.1) | dynamic-update-slice | bytes 4000004 | tf_op jit(solution)/shard_map/scatter-add | solution.py:82
  567.8 1.8 copy.44
  (67 shorter events, 4.5 us)
Async XLA Ops:
  7.9 37.6 %all-to-all-start = ((f32[32,6,12]{2,1,0:T(8,128)}), f32[32,6,12]{2,1,0:T(8,128)S(1)}, u32[]{:S(2)}, u32[]{:S(2)}) async-start(f32[32,6,12]{2,1,0:T(8,128)} %stack.16), calls=%async_computation | async-start | bytes 262144 | tf_op jit(solution)/shard_map/all_to_all | solution.py:13
  18.0 253.8 %all-reduce.10.cloned.1.call-start = ((), (), s32[]{:S(2)}) async-start(), calls=%async_computation.3 | async-start | bytes 1572864 | tf_op jit(solution)/shard_map/psum | solution.py:19
  61.6 30.9 %copy-start.1 = (f32[128,64]{1,0:T(8,128)S(1)}, f32[128,64]{1,0:T(8,128)}, u32[]{:S(2)}) copy-start(f32[128,64]{1,0:T(8,128)} %pad_convert_fusion) | copy-start | bytes 98308
  278.5 1.3 copy-start
  291.4 26.6 %all-to-all-start.1 = ((f32[32,6,12]{2,1,0:T(8,128)}), f32[32,6,12]{2,1,0:T(8,128)S(1)}, u32[]{:S(2)}, u32[]{:S(2)}) async-start(f32[32,6,12]{2,1,0:T(8,128)} %stack.20), calls=%async_computation.1 | async-start | bytes 262144 | tf_op jit(solution)/shard_map/all_to_all | solution.py:13
  298.1 248.6 %all-reduce.8.cloned.1.call-start = ((), (), s32[]{:S(2)}) async-start(), calls=%async_computation.2 | async-start | bytes 1572864 | tf_op jit(solution)/shard_map/psum | solution.py:19
  334.5 30.9 %copy-start.2 = (f32[128,64]{1,0:T(8,128)S(1)}, f32[128,64]{1,0:T(8,128)}, u32[]{:S(2)}) copy-start(f32[128,64]{1,0:T(8,128)} %pad_convert_fusion) | copy-start | bytes 98308
Sparse Core Ops, SparseCore 0:
  114.7 157.0 all-reduce.9
  387.7 158.9 all-reduce.7
